TPU v7x, 256 devices: a whole 4x4x8 slice. The times are simulated.
256 devices in a mesh: cal: 64 (over z, y, core), gr: 4 (over x).
Axes of the slice: x: 4, y: 4, z: 8, core: 2. Of those that a mesh axis runs over, the one named last changes fastest.
Arguments:
- features: bfloat16 [131072, 4096], P('cal', 'gr'), may hold values from -6 to 6
- coef: bfloat16 [4096], P('gr'), may hold values from -0.09375 to 0.09375
- log_exposure: float32 [131072], P('cal'), may hold values from -0.7 to 0.7
- claims: float32 [131072], P('cal'), may hold values from 0 to 4
- cluster_id: int32 [131072], P('cal'), may hold values from 0 to 1023
- period: int32 [131072], P('cal'), may hold values from 0 to 127, as said below
- period_effect: float32 [128], replicated, may hold values from -0.5 to 0.5
Outputs:
- meat: float32 [4096, 4096], P('cal', 'gr')
Inputs may be any that keep to these rules, and one draw needn't show every extreme that they name: `period`: rows of index d of cal lie in periods d * 2 to (d + 1) * 2 - 1.
All inputs are finite; a program needn't handle non-finite values.
Results may differ from a plain program's by a relative error of at most 0.0044.
Values sent between devices are 32-bit elements; how exact they have to be, the bound alone decides.
A program may use at most 64 MiB of HBM per device.

v0:
```python
import jax
import jax.numpy as jnp
from jax import lax
from jax.sharding import PartitionSpec as P

CL_DEV = 16


def per_device(features, coef, log_exposure, claims, cluster_id, period, period_effect):
    rows_here = features.shape[0]
    width = features.shape[1]
    n_cal = lax.axis_size("cal")
    clusters = CL_DEV * n_cal
    local_lin = jnp.dot(features, coef, preferred_element_type=jnp.float32)
    linear = lax.psum(local_lin, "gr")
    periods = period_effect.shape[0]
    table = jnp.where(
        period[:, None] == jnp.arange(periods, dtype=jnp.int32)[None, :],
        period_effect[None, :],
        jnp.float32(0.0),
    )
    shift = jnp.sum(table, axis=1)
    resid = (claims - jnp.exp(linear + log_exposure + shift)).astype(jnp.bfloat16)
    block = min(512, rows_here)
    count = rows_here // block
    feats = features.reshape(count, block, width)
    res_b = resid.reshape(count, block)
    ids_b = cluster_id.reshape(count, block)
    cluster_range = jnp.arange(clusters, dtype=jnp.int32)

    def step(carry, item):
        feat_blk, res_blk, id_blk = item
        picks = jnp.where(
            id_blk[:, None] == cluster_range[None, :], res_blk[:, None], jnp.bfloat16(0.0)
        )
        term = lax.dot_general(
            picks, feat_blk, (((0,), (0,)), ((), ())), preferred_element_type=jnp.float32
        )
        return (carry + term, None)

    partial_scores, _ = lax.scan(
        step, jnp.zeros((clusters, width), jnp.float32), (feats, res_b, ids_b)
    )
    owned = lax.psum_scatter(partial_scores, "cal", scatter_dimension=0, tiled=True)
    full_scores = lax.all_gather(owned, "gr", axis=1, tiled=True)
    scale = jnp.float32(1.0) / jnp.float32(rows_here * n_cal)
    meat_block = lax.psum_scatter(
        lax.dot_general(
            full_scores,
            owned,
            (((0,), (0,)), ((), ())),
            precision=lax.Precision.HIGHEST,
            preferred_element_type=jnp.float32,
        ),
        "cal",
        scatter_dimension=0,
        tiled=True,
    )
    return meat_block * scale


def solution(mesh):
    placed = (P("cal", "gr"), P("gr"), P("cal"), P("cal"), P("cal"), P("cal"), P())
    return jax.shard_map(
        per_device, mesh=mesh, in_specs=placed, out_specs=P("cal", "gr"), check_vma=False
    )
```

profile of v0, /device:TPU:21, one launch (start us, length us, event | category | flops | bytes accessed | tf_op | source)
XLA Modules:
  0.0 410.4 jit_solution(18031180852784625165)
XLA Ops:
  6.5 0.0 copy-start
  6.5 0.0 reduce-scatter.3.cloned.1.call-start
  6.6 0.7 reshape.19
  7.3 3.4 fusion.11
  10.7 6.4 %psum.7 = f32[2048]{0:T(1024)S(1)} all-reduce(f32[2048]{0:T(1024)S(1)} %bitcast.16), channel_id=1, replica_groups=mesh['cal'=64,'gr'=4] {'gr'}, use_global_device_ids=true, to_apply=%region_0.0 | all-reduce | flops 2048 | bytes 16384 | tf_op jit(solution)/shard_map/psum | solution.py:15
  17.1 0.0 copy-done
  17.1 0.0 copy-done.4
  17.1 0.0 copy-done.1
  17.1 0.6 select_reduce_fusion
  17.7 0.0 copy-done.2
  17.8 0.0 copy-done.3
  17.8 22.3 %while.11 = (s32[]{:T(128)}, f32[1024,1024]{1,0:T(8,128)}, s32[4,512]{1,0:T(4,128)S(1)}, bf16[4,512]{1,0:T(4,128)(2,1)S(1)}, bf16[4,512,1024]{2,1,0:T(8,128)(2,1)}, /*index=5*/s32[]{:T(128)}, s32[]{:T(128)}) while((s32[]{:T(128)}, f32[1024,1024]{1,0:T(8,128)}, s32[4,512]{1,0:T(4,128)S(1)}, bf16[4,512]{1,0:T(4,128)(2,1)S(1)}, ...), condition=%wide.region_3.4_spmd.clone, body=%wide.region_2.3_spmd.clone.sunk | while | flops 1076887552 | bytes 9446507 | solution.py:41
  17.9 4.6 %select_add_fusion.2 = f32[1024,1024]{1,0:T(8,128)} fusion(f32[1024,1024]{1,0:T(8,128)} %get-tuple-element.107, pred[]{:T(512)S(6)} %compare.3, bf16[4,512,1024]{2,1,0:T(8,128)(2,1)} %get-tuple-element.117, s32[]{:T(128)S(6)} %copy.10, s32[512]{0:T(512)S(1)} %bitcast.15, bf16[512]{0:T(512)(128)(2,1)S(1)} %dynamic-slice_reduce_fusion.2), kind=kOutput, calls=%fused_computation.1.clone.1 | convolution fusion | flops 1076887552 | bytes 9440261 | tf_op jit(solution)/shard_map/while/body/eval_jaxpr/dot_general | solution.py:36
  22.5 5.9 %select_add_fusion.2 = f32[1024,1024]{1,0:T(8,128)} fusion(f32[1024,1024]{1,0:T(8,128)} %get-tuple-element.107, pred[]{:T(512)S(6)} %compare.3, bf16[4,512,1024]{2,1,0:T(8,128)(2,1)} %get-tuple-element.117, s32[]{:T(128)S(6)} %copy.10, s32[512]{0:T(512)S(1)} %bitcast.15, bf16[512]{0:T(512)(128)(2,1)S(1)} %dynamic-slice_reduce_fusion.2), kind=kOutput, calls=%fused_computation.1.clone.1 | convolution fusion | flops 1076887552 | bytes 9440261 | tf_op jit(solution)/shard_map/while/body/eval_jaxpr/dot_general | solution.py:36
  28.4 5.9 %select_add_fusion.2 = f32[1024,1024]{1,0:T(8,128)} fusion(f32[1024,1024]{1,0:T(8,128)} %get-tuple-element.107, pred[]{:T(512)S(6)} %compare.3, bf16[4,512,1024]{2,1,0:T(8,128)(2,1)} %get-tuple-element.117, s32[]{:T(128)S(6)} %copy.10, s32[512]{0:T(512)S(1)} %bitcast.15, bf16[512]{0:T(512)(128)(2,1)S(1)} %dynamic-slice_reduce_fusion.2), kind=kOutput, calls=%fused_computation.1.clone.1 | convolution fusion | flops 1076887552 | bytes 9440261 | tf_op jit(solution)/shard_map/while/body/eval_jaxpr/dot_general | solution.py:36
  34.2 5.9 %select_add_fusion.2 = f32[1024,1024]{1,0:T(8,128)} fusion(f32[1024,1024]{1,0:T(8,128)} %get-tuple-element.107, pred[]{:T(512)S(6)} %compare.3, bf16[4,512,1024]{2,1,0:T(8,128)(2,1)} %get-tuple-element.117, s32[]{:T(128)S(6)} %copy.10, s32[512]{0:T(512)S(1)} %bitcast.15, bf16[512]{0:T(512)(128)(2,1)S(1)} %dynamic-slice_reduce_fusion.2), kind=kOutput, calls=%fused_computation.1.clone.1 | convolution fusion | flops 1076887552 | bytes 9440261 | tf_op jit(solution)/shard_map/while/body/eval_jaxpr/dot_general | solution.py:36
  40.1 0.0 reduce-scatter.3.cloned.1.call-update
  40.1 0.0 reduce-scatter.5.cloned.1.call-start
  40.2 142.9 %reduce-scatter.3.cloned.1.call-done = f32[16,1024]{1,0:T(8,128)} async-done(((f32[1024,1024]{1,0:T(8,128)}), f32[16,1024]{1,0:T(8,128)}) %reduce-scatter.3.cloned.1.call-update) | async-done | bytes 65552 | tf_op jit(solution)/shard_map/reduce_scatter | solution.py:44
  183.1 8.6 %all_gather.3 = f32[16,4096]{1,0:T(8,128)S(1)} all-gather(f32[16,1024]{1,0:T(8,128)} %reduce-scatter.3.cloned.1.call-done), channel_id=1, replica_groups=mesh['cal'=64,'gr'=4] {'gr'}, dimensions={1}, use_global_device_ids=true | all-gather | bytes 327680 | tf_op jit(solution)/shard_map/all_gather | solution.py:45
  191.6 16.7 %fusion.12 = f32[4096,1024]{1,0:T(8,128)} fusion(f32[16,4096]{1,0:T(8,128)S(1)} %all_gather.3, f32[16,1024]{1,0:T(8,128)} %reduce-scatter.3.cloned.1.call-done), kind=kOutput, calls=%fused_computation.18 | convolution fusion | flops 805306368 | bytes 17104896 | tf_op jit(solution)/shard_map/dot_general | solution.py:48
  208.3 0.0 reduce-scatter.5.cloned.1.call-update
  208.4 193.5 %reduce-scatter.5.cloned.1.call-done = f32[64,1024]{1,0:T(8,128)} async-done(((f32[4096,1024]{1,0:T(8,128)}), f32[64,1024]{1,0:T(8,128)}) %reduce-scatter.5.cloned.1.call-update) | async-done | bytes 262160 | tf_op jit(solution)/shard_map/reduce_scatter | solution.py:47
  401.9 1.7 broadcast_multiply_fusion
  (16 shorter events, 0.2 us)
Async XLA Ops:
  6.5 10.5 %copy-start = (s32[2048]{0:T(1024)S(1)}, s32[2048]{0:T(1024)}, u32[]{:S(2)}) copy-start(s32[2048]{0:T(1024)} %param.13) | copy-start | bytes 24580
  6.5 10.6 %copy-start.4 = (f32[128]{0:T(128)S(1)}, f32[128]{0:T(128)}, u32[]{:S(2)}) copy-start(f32[128]{0:T(128)} %param.15) | copy-start | bytes 1540
  6.5 10.6 %copy-start.1 = (s32[2048]{0:T(1024)S(1)}, s32[2048]{0:T(1024)}, u32[]{:S(2)}) copy-start(s32[2048]{0:T(1024)} %param.14) | copy-start | bytes 24580
  6.5 11.2 %copy-start.2 = (f32[2048]{0:T(1024)S(1)}, f32[2048]{0:T(1024)}, u32[]{:S(2)}) copy-start(f32[2048]{0:T(1024)} %param.12) | copy-start | bytes 24580
  6.5 11.2 %copy-start.3 = (f32[2048]{0:T(1024)S(1)}, f32[2048]{0:T(1024)}, u32[]{:S(2)}) copy-start(f32[2048]{0:T(1024)} %param.11) | copy-start | bytes 24580
  6.5 176.5 %reduce-scatter.3.cloned.1.call-start = ((), (), s32[]{:S(2)}) async-start(), calls=%async_computation.2 | async-start | bytes 4259840 | tf_op jit(solution)/shard_map/reduce_scatter | solution.py:44
  40.1 361.7 %reduce-scatter.5.cloned.1.call-start = ((), (), s32[]{:S(2)}) async-start(), calls=%async_computation.3 | async-start | bytes 17039360 | tf_op jit(solution)/shard_map/reduce_scatter | solution.py:47
Sparse Core Ops, SparseCore 0:
  40.3 142.7 reduce-scatter.2
  208.5 193.3 reduce-scatter.4
where the time goes:
time: 416 us; the launch traced here: 410 us
  waiting for transfers between devices  336 us (81%)
  matrix products  42.2 us (10%)
  blocking collectives  15 us (4%)
  between operations  13.5 us (3%)
    reduce_scatter x1, waiting for transfers between devices, per_device(): lax.psum_scatter(lax.dot_general(full_scores, owned, (((0,), (0,)), ((),...  194 us
    reduce_scatter x1, waiting for transfers between devices, per_device(): lax.psum_scatter(partial_scores, 'cal', scatter_dimension=0, tiled=True)  143 us
    dot_general x4, matrix products, step(): lax.dot_general(picks, feat_blk, (((0,), (0,)), ((), ())), preferred_elem...  22.2 us
    dot_general x1, matrix products, per_device(): lax.dot_general(full_scores, owned, (((0,), (0,)), ((), ())), precision=l...  16.7 us
    all_gather x1, blocking collectives, per_device(): full_scores = lax.all_gather(owned, 'gr', axis=1, tiled=True)  8.57 us
  transfers between devices with their start and end apart: 2, of which 2 were waited for; matrix products, arithmetic and copies ran while one was open for 0% of the time, Pallas kernels for 0%

commit v1 on v0

v1 whole, which is shorter than its diff:
```python
import functools
import jax
import jax.numpy as jnp
from jax import lax
from jax.experimental import pallas as pl
from jax.experimental.pallas import tpu as pltpu
from jax.sharding import PartitionSpec as P

MESH = pl.DeviceIdType.MESH
LANES = 128
NY = 4
SLICES = 2


def meat_kernel(
    nz, ny, nx,
    feat_hbm, coef_ref, logexp_ref, claims_ref, ids_ref, period_ref, eff_ref,
    out_ref,
    fbuf, lin, onehot, acc, give, take, rb1, rb2, full, lhs, part, part_in,
    load_sem, lin_ssem, lin_rsem, d2d_ssem, d2d_rsem,
    ring_ssem, ring_rsem, lhs_ssem, lhs_rsem, part_ssem, part_rsem,
):
    rows, width = feat_hbm.shape
    half = acc.shape[1]
    nchunk = acc.shape[0]
    tiles = fbuf.shape[0]
    tile_w = fbuf.shape[2]
    per_tile = tile_w // LANES
    span = half // SLICES
    cal = lax.axis_index("cal")
    x = lax.axis_index("gr")
    core = lax.rem(cal, 2)
    y = lax.rem(cal // 2, ny)
    z = cal // (2 * ny)

    def dev(z_, y_, core_, x_):
        return ((z_ * ny + y_) * 2 + core_, x_)

    def z_at(k):
        return dev(lax.rem(z + k + nz, nz), y, core, x)

    def y_at(k):
        return dev(z, lax.rem(y + k + ny, ny), core, x)

    partner = dev(z, y, 1 - core, x)

    def x_at(k):
        return (cal, lax.rem(x + k, nx))

    barrier = pltpu.get_barrier_semaphore()
    greet = [partner, z_at(1), z_at(-1), y_at(1), y_at(-1)] + [x_at(k) for k in range(1, nx)]
    for other in greet:
        pl.semaphore_signal(barrier, inc=1, device_id=other, device_id_type=MESH)

    def load(t):
        return pltpu.make_async_copy(
            feat_hbm.at[:, pl.ds(t * tile_w, tile_w)], fbuf.at[t], load_sem.at[t]
        )

    for t in range(tiles):
        load(t).start()
    total = None
    for t in range(tiles):
        load(t).wait()
        weights = jnp.broadcast_to(coef_ref[:, t * tile_w : (t + 1) * tile_w], (16, tile_w))
        term = lax.dot_general(
            weights, fbuf[t], (((1,), (1,)), ((), ())), preferred_element_type=jnp.float32
        )
        total = term if total is None else total + term
    lin[x] = total[0:1, :]

    pl.semaphore_wait(barrier, len(greet))

    def lin_copy(k):
        return pltpu.make_async_remote_copy(
            src_ref=lin.at[x], dst_ref=lin.at[x],
            send_sem=lin_ssem.at[k - 1], recv_sem=lin_rsem.at[k - 1],
            device_id=x_at(k), device_id_type=MESH,
        )

    def lin_arrival(k):
        origin = lax.rem(x - k + nx, nx)
        return pltpu.make_async_remote_copy(
            src_ref=lin.at[origin], dst_ref=lin.at[origin],
            send_sem=lin_ssem.at[k - 1], recv_sem=lin_rsem.at[k - 1],
            device_id=x_at(k), device_id_type=MESH,
        )

    for k in range(1, nx):
        lin_copy(k).start()
    first = cal * 2
    spots = lax.broadcasted_iota(jnp.int32, eff_ref.shape, 1)
    low = jnp.sum(jnp.where(spots == first, eff_ref[...], 0.0), axis=1, keepdims=True)
    high = jnp.sum(jnp.where(spots == first + 1, eff_ref[...], 0.0), axis=1, keepdims=True)
    shift = jnp.where(
        period_ref[...] == first, low, jnp.where(period_ref[...] == first + 1, high, 0.0)
    )
    for k in range(1, nx):
        lin_arrival(k).wait_recv()
    linear = lin[0]
    for k in range(1, nx):
        linear = linear + lin[k]
    resid = (claims_ref[...] - jnp.exp(linear + logexp_ref[...] + shift)).astype(jnp.bfloat16)
    resid = resid.astype(jnp.float32)
    ids = ids_ref[...]
    block = 64

    def pick(b, carry):
        base = pl.multiple_of(b * block, block)
        names = base + lax.broadcasted_iota(jnp.int32, (block, rows), 0)
        onehot[pl.ds(base, block), :] = jnp.where(names == ids, resid, 0.0).astype(jnp.bfloat16)
        return carry

    lax.fori_loop(0, 2 * half // block, pick, 0)

    per_z = nz // tiles
    per_y = ny // tiles if ny >= tiles else 1

    def anchor(which):
        return jnp.where(which == 0, z // per_z, y // per_y)

    def scores(which, t):
        picked = onehot[pl.ds(pl.multiple_of(which * half, half), half), :]
        return jnp.dot(picked, fbuf[t], preferred_element_type=jnp.float32)

    order = (2, 1, 3, 0)

    def swap(i, t):
        return pltpu.make_async_remote_copy(
            src_ref=give.at[pl.ds(t * per_tile, per_tile)],
            dst_ref=take.at[pl.ds(t * per_tile, per_tile)],
            send_sem=d2d_ssem.at[i], recv_sem=d2d_rsem.at[i],
            device_id=partner, device_id_type=MESH,
        )

    def theirs(i):
        return lax.rem(anchor(1 - core) + order[i], tiles)

    def mine(i):
        return lax.rem(anchor(core) + order[i], tiles)

    for i in range(tiles):
        t = theirs(i)
        res = scores(1 - core, t)
        for q in range(per_tile):
            give[t * per_tile + q] = res[:, q * LANES : (q + 1) * LANES]
        swap(i, t).start()

    def own_tile(i):
        t = mine(i)
        res = scores(core, t)
        swap(i, t).wait_recv()
        for q in range(per_tile):
            c = t * per_tile + q
            acc[c] = res[:, q * LANES : (q + 1) * LANES] + take[c]

    class Plan:
        def __init__(self, n1, n2, p1, p2, at1, at2):
            self.n = (n1, n2)
            self.p = (p1, p2)
            self.at = (at1, at2)
            self.w = nchunk // n1
            self.piece = span // n2

        def hops(self, axis, u, d):
            n = self.n[axis]
            return n // 2 if u % 2 == d else n // 2 - 1

        def chunk(self, ref, axis, u, owner):
            if axis == 0:
                return ref.at[pl.ds(owner * self.w, self.w), pl.ds(u * span, span), :]
            row = pl.multiple_of(u * span + owner * self.piece, self.piece)
            return ref.at[pl.ds(self.p[0] * self.w, self.w), pl.ds(row, self.piece), :]

        def slot(self, axis, u, d, s):
            if axis == 0:
                return rb1.at[u, d, pl.ds(s * self.w, self.w)]
            return rb2.at[u, d, pl.ds(0, self.w), pl.ds(s * self.piece, self.piece)]

        def name(self, axis, k):
            return lax.rem(self.p[axis] + k + self.n[axis], self.n[axis])

        def reduce_copy(self, axis, u, d, s):
            sign = 1 if d == 0 else -1
            h = self.hops(axis, u, d)
            if s == 0:
                src = self.chunk(acc, axis, u, self.name(axis, sign * h))
            else:
                src = self.slot(axis, u, d, s - 1)
            return pltpu.make_async_remote_copy(
                src_ref=src, dst_ref=self.slot(axis, u, d, s),
                send_sem=ring_ssem.at[axis, u, d, s], recv_sem=ring_rsem.at[axis, u, d, s],
                device_id=self.at[axis](sign), device_id_type=MESH,
            )

        def reduce_step(self, axis, u, d, s):
            if s >= self.hops(axis, u, d):
                return
            if s > 0:
                sign = 1 if d == 0 else -1
                h = self.hops(axis, u, d)
                self.reduce_copy(axis, u, d, s - 1).wait_recv()
                here = self.slot(axis, u, d, s - 1)
                here[...] += self.chunk(acc, axis, u, self.name(axis, sign * (h - s)))[...]
            self.reduce_copy(axis, u, d, s).start()

        def reduce_end(self, axis, u):
            value = self.chunk(acc, axis, u, self.p[axis])[...]
            for d in (1, 0) if u % 2 == 0 else (0, 1):
                h = self.hops(axis, u, d)
                if h:
                    self.reduce_copy(axis, u, d, h - 1).wait_recv()
                    value = value + self.slot(axis, u, d, h - 1)[...]
            target = acc if axis == 0 else full
            self.chunk(target, axis, u, self.p[axis])[...] = value

        def gather_copy(self, axis, u, d, s, back):
            sign = 1 if d == 0 else -1
            there = self.chunk(full, axis, u, self.name(axis, -sign * (s + back)))
            return pltpu.make_async_remote_copy(
                src_ref=there, dst_ref=there,
                send_sem=ring_ssem.at[2 + axis, u, d, s],
                recv_sem=ring_rsem.at[2 + axis, u, d, s],
                device_id=self.at[axis](sign), device_id_type=MESH,
            )

        def gather_step(self, axis, u, d, s):
            if s >= self.hops(axis, u, d):
                return
            if s > 0:
                self.gather_copy(axis, u, d, s - 1, 1).wait_recv()
            self.gather_copy(axis, u, d, s, 0).start()

        def gather_end(self, axis, u):
            for d in (0, 1):
                h = self.hops(axis, u, d)
                if h:
                    self.gather_copy(axis, u, d, h - 1, 1).wait_recv()

        def flows(self, axis):
            pairs = [(u, d) for u in range(SLICES) for d in (0, 1)]
            return sorted(pairs, key=lambda f: -self.hops(axis, *f))

        def longest(self, axis):
            return self.n[axis] // 2

        def start_long(self):
            for u, d in self.flows(0):
                if self.hops(0, u, d) == self.longest(0):
                    self.reduce_step(0, u, d, 0)

        def start_short(self):
            for u, d in self.flows(0):
                if self.hops(0, u, d) < self.longest(0):
                    self.reduce_step(0, u, d, 0)

        def middle(self):
            for s in range(1, self.longest(0)):
                for u, d in self.flows(0):
                    self.reduce_step(0, u, d, s)
            for u in range(SLICES):
                self.reduce_end(0, u)
                for d in (0, 1):
                    self.reduce_step(1, u, d, 0)
            for s in range(1, self.longest(1)):
                for u, d in self.flows(1):
                    self.reduce_step(1, u, d, s)
            for u in range(SLICES):
                self.reduce_end(1, u)
                for d in (0, 1):
                    self.gather_step(1, u, d, 0)
            for s in range(1, self.longest(1)):
                for u, d in self.flows(1):
                    self.gather_step(1, u, d, s)
            for u in range(SLICES):
                self.gather_end(1, u)
                for d in (0, 1):
                    self.gather_step(0, u, d, 0)
            for s in range(1, self.longest(0)):
                for u, d in self.flows(0):
                    self.gather_step(0, u, d, s)

        def drain(self):
            for axis in (0, 1):
                for u, d in self.flows(axis):
                    for s in range(self.hops(axis, u, d)):
                        self.reduce_copy(axis, u, d, s).wait_send()
                        self.gather_copy(axis, u, d, s, 0).wait_send()

    plans = (Plan(nz, ny, z, y, z_at, y_at), Plan(ny, nz, y, z, y_at, z_at))

    def each(act):
        for which in (0, 1):
            @pl.when(core == which)
            def _():
                act(plans[which])

    own_tile(0)
    each(lambda plan: plan.start_long())
    own_tile(1)
    own_tile(2)
    each(lambda plan: plan.start_short())
    own_tile(3)
    each(lambda plan: plan.middle())

    chip = z * ny + y
    home = chip * LANES // width
    place = lax.rem(chip, width // LANES)
    chip_rows = LANES

    def lhs_copy(u, k):
        return pltpu.make_async_remote_copy(
            src_ref=full.at[place, pl.ds(u * span, span), :],
            dst_ref=lhs.at[pl.ds(u * span, span), :],
            send_sem=lhs_ssem.at[u, k - 1], recv_sem=lhs_rsem.at[u],
            device_id=x_at(k), device_id_type=MESH,
        )

    for u in range(SLICES):
        each(lambda plan: plan.gather_end(0, u))

        @pl.when(x == home)
        def _():
            for k in range(1, nx):
                lhs_copy(u, k).start()
            lhs[pl.ds(u * span, span), :] = full[place, pl.ds(u * span, span), :]

    for u in range(SLICES):
        @pl.when(x != home)
        def _():
            lhs_copy(u, 1).wait_recv()

        left = lhs[pl.ds(u * span, span), :].T
        for t in range(tiles):
            right = jnp.concatenate(
                [full[t * per_tile + q, pl.ds(u * span, span), :] for q in range(per_tile)], axis=1
            )
            term = jnp.dot(
                left, right, precision=lax.Precision.HIGHEST, preferred_element_type=jnp.float32
            )
            cols = pl.ds(t * tile_w, tile_w)
            if u == 0:
                part[:, cols] = term
            else:
                part[:, cols] += term

    keep = chip_rows // 2
    trade = pltpu.make_async_remote_copy(
        src_ref=part.at[pl.ds(pl.multiple_of((1 - core) * keep, keep), keep), :],
        dst_ref=part_in,
        send_sem=part_ssem, recv_sem=part_rsem,
        device_id=partner, device_id_type=MESH,
    )
    trade.start()
    for k in range(1, nx):
        lin_copy(k).wait_send()
    for i in range(tiles):
        swap(i, theirs(i)).wait_send()
    each(lambda plan: plan.drain())

    @pl.when(x == home)
    def _():
        for u in range(SLICES):
            for k in range(1, nx):
                lhs_copy(u, k).wait_send()

    trade.wait_recv()
    count = rows * nz * ny * 2
    scale = jnp.float32(1.0) / jnp.float32(count)
    own = part[pl.ds(pl.multiple_of(core * keep, keep), keep), :]
    out_ref[...] = (own + part_in[...]) * scale
    trade.wait_send()


def per_device(clusters, ny, features, coef, log_exposure, claims, cluster_id, period, period_effect):
    rows, width = features.shape
    nx = lax.axis_size("gr")
    nz = lax.axis_size("cal") // (2 * ny)
    half = clusters // 2
    span = half // SLICES
    nchunk = width // LANES
    tiles = 4
    tile_w = width // tiles
    f32 = jnp.float32
    dma = pltpu.SemaphoreType.DMA
    depth = max(nchunk // 2, 1)
    vm = pl.BlockSpec(memory_space=pltpu.VMEM)
    return pl.pallas_call(
        functools.partial(meat_kernel, nz, ny, nx),
        out_shape=jax.ShapeDtypeStruct((LANES // 2, width), f32),
        in_specs=[pl.BlockSpec(memory_space=pl.ANY)] + [vm] * 6,
        out_specs=vm,
        scratch_shapes=[
            pltpu.VMEM((tiles, rows, tile_w), jnp.bfloat16),
            pltpu.VMEM((nx, 1, rows), f32),
            pltpu.VMEM((clusters, rows), jnp.bfloat16),
            pltpu.VMEM((nchunk, half, LANES), f32),
            pltpu.VMEM((nchunk, half, LANES), f32),
            pltpu.VMEM((nchunk, half, LANES), f32),
            pltpu.VMEM((SLICES, 2, depth, span, LANES), f32),
            pltpu.VMEM((SLICES, 2, 2, span // 2, LANES), f32),
            pltpu.VMEM((nchunk, half, LANES), f32),
            pltpu.VMEM((half, LANES), f32),
            pltpu.VMEM((LANES, width), f32),
            pltpu.VMEM((LANES // 2, width), f32),
            dma((tiles,)),
            dma((nx - 1,)),
            dma((nx - 1,)),
            dma((tiles,)),
            dma((tiles,)),
            dma((4, SLICES, 2, 4)),
            dma((4, SLICES, 2, 4)),
            dma((SLICES, nx - 1)),
            dma((SLICES,)),
            dma,
            dma,
        ],
        compiler_params=pltpu.CompilerParams(
            collective_id=0, has_side_effects=True, vmem_limit_bytes=60 * 1024 * 1024
        ),
    )(
        features,
        coef.reshape(1, width),
        log_exposure.reshape(1, rows),
        claims.reshape(1, rows),
        cluster_id.reshape(1, rows),
        period.reshape(1, rows),
        period_effect.reshape(1, -1),
    )


def solution(mesh, clusters=1024, ny=NY):
    placed = (P("cal", "gr"), P("gr"), P("cal"), P("cal"), P("cal"), P("cal"), P())
    return jax.shard_map(
        functools.partial(per_device, clusters, ny),
        mesh=mesh, in_specs=placed, out_specs=P("cal", "gr"), check_vma=False,
    )
```

time: 416 us -> 82.3 us (0.20); the launches traced: 410 us -> 82.1 us
  waiting for transfers between devices: 336 us -> 0 us
  Pallas kernels: 0 us -> 79.1 us
  matrix products: 42.2 us -> 0 us
  blocking collectives: 15 us -> 0 us
  between operations: 13.5 us -> 0.01 us
    reduce_scatter x2 -> x0, waiting for transfers between devices: 336 us -> none  [the longest x1 194 us: per_device(): lax.psum_scatter(lax.dot_general(full_scores, owned, (((0,), (0,)), ((),...]
    pallas_call x0 -> x1, Pallas kernels: none -> 79.1 us  [per_device(): pl.pallas_call(functools.partial(meat_kernel, nz, ny, nx), out_shape=jax....]
    dot_general x6 -> x0, matrix products: 42.2 us -> none  [the longest x4 22.2 us: step(): lax.dot_general(picks, feat_blk, (((0,), (0,)), ((), ())), preferred_elem...]
    all_gather x1 -> x0, blocking collectives: 8.57 us -> none  [per_device(): full_scores = lax.all_gather(owned, 'gr', axis=1, tiled=True)]
    psum x1 -> x0, blocking collectives: 6.4 us -> none  [per_device(): linear = lax.psum(local_lin, 'gr')]
  transfers between devices with their start and end apart: 2 -> 0, of which waited for: 2 -> 0; matrix products, arithmetic and copies ran while one was open for 0% -> 0% of each run, Pallas kernels for 0% -> 0%
where the time goes in v1:
time: 82.3 us; the launch traced here: 82.1 us
  Pallas kernels  79.1 us (96%)
  local copies, waits for them, and re-layouts  2.95 us (4%)
    pallas_call x1, Pallas kernels, per_device(): pl.pallas_call(functools.partial(meat_kernel, nz, ny, nx), out_shape=jax....  79.1 us
    unnamed x1, local copies, waits for them, and re-layouts  1.67 us

profile of v1, /device:TPU:21, one launch (start us, length us, event | category | flops | bytes accessed | tf_op | source)
XLA Modules:
  0.0 82.1 jit_solution(12220225573826274829)
XLA Ops:
  0.0 1.3 %reshape.18.coef_ref = bf16[1,1024]{1,0:T(2,128)(2,1)} reshape(bf16[1024]{0:T(1024)(128)(2,1)} %param.8) | data formatting | bytes 4096 | tf_op jit(solution)/shard_map/reshape | solution.py:423
  1.3 79.1 %shard_map.73 = f32[64,1024]{1,0:T(8,128)} custom-call(bf16[2048,1024]{1,0:T(8,128)(2,1)} %feat_hbm.1, bf16[1,1024]{1,0:T(2,128)(2,1)} %reshape.18.coef_ref, f32[1,2048]{1,0:T(1,128)} %bitcast.5, f32[1,2048]{1,0:T(1,128)} %bitcast.6, s32[1,2048]{1,0:T(1,128)} %bitcast.7, s32[1,2048]{1,0:T(1,128)} %bitcast.8, f32[1,128]{1,0:T(1,128)} %bitcast.9), custom_call_target="tpu_custom_call" | custom-call | tf_op jit(solution)/shard_map/pallas_call | solution.py:388
  80.4 1.7 %copy.9 = f32[64,1024]{1,0:T(8,128)} copy(f32[64,1024]{1,0:T(8,128)} %shard_map.73) | data formatting | bytes 524288
